TPU v7x, 512 devices: a whole 4x8x8 slice. The times are simulated.
512 devices in a mesh: space: 64 (over y, x, z_hi), chan: 8 (over z_lo, core).
Axes of the slice: x: 4, y: 8, z: 8 (z_hi: 2, z_lo: 4; z = z_hi * 4 + z_lo), core: 2. Of those that a mesh axis runs over, the one named last changes fastest.
Arguments:
- source: bfloat16 [512, 192, 128], P('chan', 'space'), may hold values from -6 to 6
- kernel: bfloat16 [7, 7, 512, 512], P(None, None, 'chan'), may hold values from -0.0390625 to 0.0390625
Outputs:
- image: bfloat16 [512, 192, 128], P('chan', 'space')
All inputs are finite; a program needn't handle non-finite values.
Results may differ from a plain program's by a relative error of at most 0.001.
Values may be sent and summed in bfloat16 or wider, within the bound.
A program may use at most 64 MiB of HBM per device.

v0:
```python
import jax
import jax.numpy as jnp
from jax import lax
from jax.sharding import PartitionSpec as P

OFF = 7


def padded_2(array, sides, width):
    for axis, dim in sides:
        devices, length = (lax.axis_size(axis), array.shape[dim])
        up = [(i, (i + 1) % devices) for i in range(devices - 1)]
        down = [(j, i) for i, j in up]
        last = lax.slice_in_dim(array, length - width, length, axis=dim)
        initial = lax.slice_in_dim(array, 0, width, axis=dim)
        before = lax.ppermute(last, axis, up)
        after = lax.ppermute(initial, axis, down)
        array = jnp.concatenate([before, array, after], axis=dim)
    return array


def correlate(kernel, padded, height):
    reach = (OFF - 1) // 2
    width_cols = padded.shape[2]
    widened = jnp.pad(padded, ((0, 0), (0, 0), (reach, reach)))
    total = jnp.zeros((kernel.shape[2], height, width_cols), jnp.float32)
    for row_shift in range(OFF):
        window = widened[:, row_shift : row_shift + height, :]
        stacked = jnp.stack(
            [window[:, :, col_shift : col_shift + width_cols] for col_shift in range(OFF)]
        )
        weights = kernel[row_shift]
        total = total + jnp.einsum(
            "boc,bcxy->oxy", weights, stacked, preferred_element_type=jnp.float32
        )
    return total


def shards(source, kernel):
    reach = (OFF - 1) // 2
    height = source.shape[1]
    rimmed = padded_2(source, (("space", 1),), reach)
    coupled = correlate(kernel, lax.all_gather(rimmed, "chan", axis=0, tiled=True), height)
    return (source.astype(jnp.float32) - coupled).astype(jnp.bfloat16)


def solution(mesh):
    placed = (P("chan", "space", None), P(None, None, "chan", None))
    return jax.shard_map(
        shards, mesh=mesh, in_specs=placed, out_specs=P("chan", "space", None), check_vma=False
    )
```

profile of v0, /device:TPU:2, one launch (start us, length us, event | category | flops | bytes accessed | tf_op | source)
XLA Modules:
  0.0 92.9 jit_solution(15703168403566414398)
XLA Ops:
  6.5 10.9 %collective-permute-start = (bf16[64,3,128]{2,0,1:T(8,128)(2,1)}, bf16[64,3,128]{2,0,1:T(8,128)(2,1)S(1)}, u32[]{:S(2)}, u32[]{:S(2)}) collective-permute-start(bf16[64,3,128]{2,0,1:T(8,128)(2,1)} %param.2), channel_id=1, source_target_pairs={{0,8},{8,16},{16,24},{24,32},{32,40},{40,48},{48,56},{56,64},{64,7... | collective-permute-start | bytes 147464 | tf_op jit(solution)/shard_map/ppermute | solution.py:16
  17.5 1.9 %collective-permute-start.1 = (bf16[64,3,128]{2,0,1:T(8,128)(2,1)}, bf16[64,3,128]{2,0,1:T(8,128)(2,1)S(1)}, u32[]{:S(2)}, u32[]{:S(2)}) collective-permute-start(bf16[64,3,128]{2,0,1:T(8,128)(2,1)} %param.2), channel_id=1, source_target_pairs={{8,0},{16,8},{24,16},{32,24},{40,32},{48,40},{56,48},{64,56},{72,6... | collective-permute-start | bytes 147464 | tf_op jit(solution)/shard_map/ppermute | solution.py:17
  19.4 1.1 %collective-permute-done = bf16[64,3,128]{2,0,1:T(8,128)(2,1)S(1)} collective-permute-done((bf16[64,3,128]{2,0,1:T(8,128)(2,1)}, bf16[64,3,128]{2,0,1:T(8,128)(2,1)S(1)}, u32[]{:S(2)}, u32[]{:S(2)}) %collective-permute-start) | collective-permute-done | bytes 49184 | tf_op jit(solution)/shard_map/ppermute | solution.py:16
  20.5 7.9 %collective-permute-done.1 = bf16[64,3,128]{2,0,1:T(8,128)(2,1)S(1)} collective-permute-done((bf16[64,3,128]{2,0,1:T(8,128)(2,1)}, bf16[64,3,128]{2,0,1:T(8,128)(2,1)S(1)}, u32[]{:S(2)}, u32[]{:S(2)}) %collective-permute-start.1) | collective-permute-done | bytes 49184 | tf_op jit(solution)/shard_map/ppermute | solution.py:17
  28.4 1.5 %pad_maximum_fusion = bf16[64,9,128]{2,0,1:T(8,128)(2,1)} fusion(bf16[64,3,128]{2,0,1:T(8,128)(2,1)S(1)} %collective-permute-done.1, bf16[64,3,128]{2,0,1:T(8,128)(2,1)} %param.2, bf16[64,3,128]{2,0,1:T(8,128)(2,1)S(1)} %collective-permute-done), kind=kLoop, calls=%fused_computation.170 | loop fusion | flops 147456 | bytes 294912 | tf_op jit(solution)/shard_map/concatenate | solution.py:18
  29.9 39.3 %all-gather.2.cloned.1.call-done = bf16[512,9,128]{2,0,1:T(8,128)(2,1)} async-done(((bf16[64,9,128]{2,0,1:T(8,128)(2,1)}), bf16[512,9,128]{2,0,1:T(8,128)(2,1)}) %all-gather.2.cloned.1.call-update) | async-done | bytes 1179664 | tf_op jit(solution)/shard_map/all_gather | solution.py:43
  69.2 1.3 %fusion.36 = bf16[7,512,3,128]{3,1,2,0:T(8,128)(2,1)S(1)} fusion(bf16[512,9,128]{2,0,1:T(8,128)(2,1)} %all-gather.2.cloned.1.call-done), kind=kLoop, calls=%fused_computation.85 | loop fusion | bytes 1572864
  70.5 1.2 %fusion.38 = bf16[7,512,3,128]{3,1,2,0:T(8,128)(2,1)S(1)} fusion(bf16[7,512,3,128]{3,1,2,0:T(8,128)(2,1)S(1)} %fusion.36, bf16[512,9,128]{2,0,1:T(8,128)(2,1)} %all-gather.2.cloned.1.call-done), kind=kLoop, calls=%fused_computation.87 | loop fusion | bytes 1572864
  71.7 0.2 fusion.40
  72.0 0.2 fusion.42
  72.2 0.2 fusion.44
  72.5 0.8 fusion.46
  73.3 0.2 fusion.50
  73.8 0.2 fusion.54
  74.3 1.0 %fusion.58 = (bf16[7,512,3,128]{3,1,2,0:T(8,128)(2,1)S(1)}, bf16[7,512,3,128]{3,1,2,0:T(8,128)(2,1)S(1)}, bf16[7,512,3,128]{3,1,2,0:T(8,128)(2,1)S(1)}, bf16[7,5...) fusion(bf16[7,512,3,128]{3,1,2,0:T(8,128)(2,1)S(1)} %fusion.56, bf16[512,9,128]{2,0,1:T(8,128)(2,1)S(1)} %copy-done, ...), kind=kLoop, calls=%fused_computation.107 | loop fusion | bytes 3145728 | tf_op jit(solution)/shard_map/stack | solution.py:29
  75.3 0.2 fusion.64
  75.5 0.2 fusion.66
  75.8 0.2 fusion.68
  76.0 0.8 fusion.70
  77.1 0.4 fusion.80
  77.5 0.6 fusion.82
  78.1 0.2 fusion.92
  78.3 0.4 fusion.94
  78.7 0.2 fusion.106
  79.0 1.0 %copy-done.1 = bf16[7,7,64,512]{3,2,1,0:T(8,128)(2,1)S(1)} copy-done((bf16[7,7,64,512]{3,2,1,0:T(8,128)(2,1)S(1)}, bf16[7,7,64,512]{3,2,1,0:T(8,128)(2,1)}, u32[]{:S(2)}) %copy-start.1) | copy-done | bytes 3211288
  80.0 0.6 convolution_bitcast_fusion
  80.6 0.6 convolution_bitcast_fusion.1
  81.1 0.6 convolution_bitcast_fusion.2
  81.7 0.6 convolution_bitcast_fusion.3
  82.3 0.6 convolution_bitcast_fusion.4
  82.8 0.6 convolution_bitcast_fusion.5
  84.8 1.2 %fusion.8 = bf16[64,3,128]{2,0,1:T(8,128)(2,1)} fusion(f32[3,128,64]{1,2,0:T(8,128)S(1)} %convolution_bitcast_fusion, f32[3,128,64]{1,2,0:T(8,128)S(1)} %convolution_bitcast_fusion.1, f32[3,128,64]{1,2,0:T(8,128)S(1)} %convolution_bitcast_fusion.2, f32[3,128,64]{1,2,0:T(8,128)S(1)} %convolution_bitcast_fusion.3, ...), kind=kOutput, calls=%fused_computation.57 | convolution fusion | flops 176381952 | bytes 3899392 | tf_op jit(solution)/shard_map/boc,bcxy->oxy/dot_general | solution.py:33
  (21 shorter events, 2.3 us)
Async XLA Ops:
  6.5 62.7 %all-gather.2.cloned.1.call-start = ((), (), s32[]{:S(2)}) async-start(), calls=%async_computation | async-start | bytes 1327104 | tf_op jit(solution)/shard_map/all_gather | solution.py:43
  6.5 13.9 %collective-permute-start = (bf16[64,3,128]{2,0,1:T(8,128)(2,1)}, bf16[64,3,128]{2,0,1:T(8,128)(2,1)S(1)}, u32[]{:S(2)}, u32[]{:S(2)}) collective-permute-start(bf16[64,3,128]{2,0,1:T(8,128)(2,1)} %param.2), channel_id=1, source_target_pairs={{0,8},{8,16},{16,24},{24,32},{32,40},{40,48},{48,56},{56,64},{64,7... | collective-permute-start | bytes 147464 | tf_op jit(solution)/shard_map/ppermute | solution.py:16
  17.5 11.0 %collective-permute-start.1 = (bf16[64,3,128]{2,0,1:T(8,128)(2,1)}, bf16[64,3,128]{2,0,1:T(8,128)(2,1)S(1)}, u32[]{:S(2)}, u32[]{:S(2)}) collective-permute-start(bf16[64,3,128]{2,0,1:T(8,128)(2,1)} %param.2), channel_id=1, source_target_pairs={{8,0},{16,8},{24,16},{32,24},{40,32},{48,40},{56,48},{64,56},{72,6... | collective-permute-start | bytes 147464 | tf_op jit(solution)/shard_map/ppermute | solution.py:17
  69.2 2.5 %copy-start = (bf16[512,9,128]{2,0,1:T(8,128)(2,1)S(1)}, bf16[512,9,128]{2,0,1:T(8,128)(2,1)}, u32[]{:S(2)}) copy-start(bf16[512,9,128]{2,0,1:T(8,128)(2,1)} %all-gather.2.cloned.1.call-done) | copy-start | bytes 3538948
  78.1 1.9 %copy-start.1 = (bf16[7,7,64,512]{3,2,1,0:T(8,128)(2,1)S(1)}, bf16[7,7,64,512]{3,2,1,0:T(8,128)(2,1)}, u32[]{:S(2)}) copy-start(bf16[7,7,64,512]{3,2,1,0:T(8,128)(2,1)} %param.3) | copy-start | bytes 9633796
  84.0 0.8 copy-start.2
Sparse Core Ops, SparseCore 0:
  30.0 39.1 all-gather.1
where the time goes:
time: 93.2 us; the launch traced here: 92.9 us
  waiting for transfers between devices  48.3 us (52%)
  between operations  13.6 us (15%)
  starting transfers between devices  12.8 us (14%)
  local copies, waits for them, and re-layouts  12 us (13%)
  matrix products  4.56 us (5%)
  other arithmetic  1.48 us (2%)
    all_gather x1, waiting for transfers between devices, shards(): lax.all_gather(rimmed, 'chan', axis=0, tiled=True)  39.3 us
    ppermute x1, starting transfers between devices, padded_2(): before = lax.ppermute(last, axis, up)  10.9 us
    unnamed x31, local copies, waits for them, and re-layouts  7.99 us
    ppermute x1, waiting for transfers between devices, padded_2(): after = lax.ppermute(initial, axis, down)  7.92 us
    dot_general x7, matrix products, correlate(): jnp.einsum('boc,bcxy->oxy', weights, stacked, preferred_element_type=jnp....  4.56 us
    another operation x7, local copies, waits for them, and re-layouts, correlate(): jnp.stack([window[:, :, col_shift:col_shift + width_cols] for col_shift i...  4.06 us
    ppermute x1, starting transfers between devices, padded_2(): after = lax.ppermute(initial, axis, down)  1.92 us
  transfers between devices with their start and end apart: 3, of which 3 were waited for; matrix products, arithmetic and copies ran while one was open for 0% of the time, Pallas kernels for 0%

commit v1 on v0

v1 whole, which is shorter than its diff:
```python
import functools

import jax
import jax.numpy as jnp
from jax import lax
from jax.experimental import pallas as pl
from jax.experimental.pallas import tpu as pltpu
from jax.sharding import PartitionSpec as P

OFF = 7
REACH = 3
MESH = pl.DeviceIdType.MESH


def body(rings, src, weights, out, cells, held, acc, load_sem, ring_send, ring_recv, pair_send, pair_recv, side_send, side_recv):
    space, chan = lax.axis_index("space"), lax.axis_index("chan")
    ring, half = space // 2, space % 2
    low, core = chan // 2, chan % 2
    z = half * 4 + low

    def on_ring(step):
        other = (z + step + 8) % 8
        return (ring * 2 + other // 4, (other % 4) * 2 + core)

    sibling = (space, low * 2 + 1 - core)
    forward = 1 - 2 * half
    target = (((ring + forward + rings) % rings) * 2 + half, chan)
    source = (((ring - forward + rings) % rings) * 2 + half, chan)

    load = pltpu.make_async_copy(weights, held, load_sem.at[0])
    load.start()
    mine = pltpu.make_async_copy(src, cells.at[z * 2 + core], load_sem.at[1])
    mine.start()

    barrier = pltpu.get_barrier_semaphore()
    for other in (on_ring(1), on_ring(-1), sibling, source):
        pl.semaphore_signal(barrier, inc=1, device_id=other, device_id_type=MESH)
    pl.semaphore_wait(barrier, 4)

    def slot(step):
        return ((z + step + 8) % 8) * 2 + core

    def part(ref, piece):
        return ref if piece is None else ref.at[:, pl.ds(piece * 32, 32)]

    def hop(direction, step, piece=None):
        index = slot(-direction * (step - 1))
        number = (step - 1) * 2 + (direction < 0)
        return pltpu.make_async_remote_copy(
            src_ref=part(src if step == 1 else cells.at[index], piece),
            dst_ref=part(cells.at[index], piece),
            send_sem=ring_send.at[number],
            recv_sem=ring_recv.at[number],
            device_id=on_ring(direction),
            device_id_type=MESH,
        )

    def arrived(direction, step, piece=None):
        index = slot(-direction * step)
        number = (step - 1) * 2 + (direction < 0)
        view = part(cells.at[index], piece)
        pltpu.make_async_copy(view, view, ring_recv.at[number]).wait()

    def across(index, number, from_src=False):
        return pltpu.make_async_remote_copy(
            src_ref=src if from_src else cells.at[index],
            dst_ref=cells.at[index],
            send_sem=pair_send.at[number],
            recv_sem=pair_recv.at[number],
            device_id=sibling,
            device_id_type=MESH,
        )

    def sideways(index, number):
        return pltpu.make_async_remote_copy(
            src_ref=cells.at[index],
            dst_ref=cells.at[16 + index % 8],
            send_sem=side_send.at[number],
            recv_sem=side_recv.at[number],
            device_id=target,
            device_id_type=MESH,
        )

    steps = ((1, 1), (-1, 1), (1, 2), (-1, 2), (1, 3), (-1, 3))
    hop(1, 1).start()
    hop(-1, 1).start()
    across(slot(0), 0, True).start()

    def foreign(direction, step):
        return low < step if direction > 0 else low + step > 3

    def side_arrived(direction, step, number):
        index = 16 + slot(-direction * step) % 8
        pltpu.make_async_copy(cells.at[index], cells.at[index], side_recv.at[number]).wait()
        across(index, 8 + number).start()

    for number, (direction, step) in enumerate(steps):
        arrived(direction, step)
        if step < 3:
            hop(direction, step + 1).start()
        else:
            hop(direction, 4, 0 if direction > 0 else 1).start()
        across(slot(-direction * step), 1 + number).start()

        @pl.when(foreign(direction, step))
        def _():
            sideways(slot(-direction * step), number).start()

    arrived(1, 4, 0)
    arrived(-1, 4, 1)
    sideways(slot(4), 6).start()
    across(slot(4), 7).start()
    for number, (direction, step) in enumerate(steps):

        @pl.when(foreign(direction, step))
        def _():
            side_arrived(direction, step, number)

    side_arrived(1, 4, 6)

    for number, offset in enumerate((0, -1, 1, -2, 2, -3, 3, 4)):
        index = ((z + offset + 8) % 8) * 2 + 1 - core
        pltpu.make_async_copy(cells.at[index], cells.at[index], pair_recv.at[number]).wait()
        if offset == 4:
            index = 16 + index % 8
            pltpu.make_async_copy(cells.at[index], cells.at[index], pair_recv.at[14]).wait()
        elif offset != 0:
            direction = 1 if offset < 0 else -1

            @pl.when(foreign(direction, abs(offset)))
            def _():
                side = 16 + index % 8
                pltpu.make_async_copy(cells.at[side], cells.at[side], pair_recv.at[7 + number]).wait()

    for number, (direction, step) in enumerate(steps):
        hop(direction, step).wait_send()
        across(slot(-direction * step), 1 + number).wait_send()

        @pl.when(foreign(direction, step))
        def _():
            sideways(slot(-direction * step), number).wait_send()
            across(16 + slot(-direction * step) % 8, 8 + number).wait_send()

    hop(1, 4, 0).wait_send()
    hop(-1, 4, 1).wait_send()
    across(slot(0), 0, True).wait_send()
    across(slot(4), 7).wait_send()
    sideways(slot(4), 6).wait_send()
    across(16 + slot(4) % 8, 14).wait_send()
    mine.wait()
    load.wait()

    @pl.when(jnp.logical_or(space == 0, space == rings * 2 - 1))
    def _():
        cells[pl.ds(16, 8)] = jnp.zeros((8, 3, 64, 128), jnp.bfloat16)

    bases = ((1 - half) * 16, half * 8, 8 + half * 8)
    rows = [cells[pl.ds(bases[r // 3], 8), r % 3].reshape(512, 128) for r in range(9)]
    for a in range(OFF):
        stacked = jnp.concatenate(rows[a : a + 3], axis=1)
        product = jnp.dot(held[a], stacked, preferred_element_type=jnp.float32)
        if a == 0:
            acc[...] = product
        else:
            acc[...] += product

    column = lax.broadcasted_iota(jnp.int32, (64, 128), 1)
    for i in range(3):
        total = acc[REACH * 64 : REACH * 64 + 64, i * 128 : i * 128 + 128]
        for b in range(OFF):
            if b != REACH:
                shift = b - REACH
                turned = pltpu.roll(acc[b * 64 : b * 64 + 64, i * 128 : i * 128 + 128], (-shift) % 128, 1)
                valid = column < 128 - shift if shift > 0 else column >= -shift
                total += jnp.where(valid, turned, 0.0)
        own = cells[z * 2 + core, i].astype(jnp.float32)
        out[i] = (own - total).astype(jnp.bfloat16)


def solution(mesh):
    rings = mesh.shape["space"] // 2

    def shards(source, kernel):
        rows = jnp.transpose(source, (1, 0, 2))
        weights = kernel.reshape(OFF, OFF * 64, 512)
        image = pl.pallas_call(
            functools.partial(body, rings),
            out_shape=jax.ShapeDtypeStruct(rows.shape, jnp.bfloat16),
            in_specs=[pl.BlockSpec(memory_space=pl.ANY)] * 2,
            out_specs=pl.BlockSpec(memory_space=pltpu.VMEM),
            scratch_shapes=[
                pltpu.VMEM((24, 3, 64, 128), jnp.bfloat16),
                pltpu.VMEM(weights.shape, jnp.bfloat16),
                pltpu.VMEM((OFF * 64, 384), jnp.float32),
                pltpu.SemaphoreType.DMA((2,)),
                pltpu.SemaphoreType.DMA((8,)),
                pltpu.SemaphoreType.DMA((8,)),
                pltpu.SemaphoreType.DMA((15,)),
                pltpu.SemaphoreType.DMA((15,)),
                pltpu.SemaphoreType.DMA((7,)),
                pltpu.SemaphoreType.DMA((7,)),
            ],
            compiler_params=pltpu.CompilerParams(
                collective_id=0, has_side_effects=True, vmem_limit_bytes=56 * 1024 * 1024
            ),
        )(rows, weights)
        return jnp.transpose(image, (1, 0, 2))

    placed = (P("chan", "space", None), P(None, None, "chan", None))
    return jax.shard_map(
        shards, mesh=mesh, in_specs=placed, out_specs=P("chan", "space", None), check_vma=False
    )
```

time: 93.2 us -> 37.2 us (0.40)
  the two profiles are of different devices: /device:TPU:2 before, /device:TPU:1 now
where the time goes in v1:
time: 37.2 us; the launch traced here: 37 us
  Pallas kernels  35.6 us (96%)
  local copies, waits for them, and re-layouts  1.42 us (4%)
    pallas_call x1, Pallas kernels, shards(): pl.pallas_call(functools.partial(body, rings), out_shape=jax.ShapeDtypeSt...  35.6 us
    unnamed x1, local copies, waits for them, and re-layouts  1.42 us

profile of v1, /device:TPU:1, one launch (start us, length us, event | category | flops | bytes accessed | tf_op | source)
XLA Modules:
  0.0 37.0 jit_solution(3778259619662934920)
XLA Ops:
  0.0 35.6 %shard_map.28 = bf16[3,64,128]{2,1,0:T(8,128)(2,1)} custom-call(bf16[3,64,128]{2,1,0:T(8,128)(2,1)} %bitcast.5, bf16[7,448,512]{2,1,0:T(8,128)(2,1)} %bitcast.3), custom_call_target="tpu_custom_call" | custom-call | tf_op jit(solution)/shard_map/pallas_call | solution.py:186
  35.6 1.4 %copy.4 = bf16[64,3,128]{2,0,1:T(8,128)(2,1)} copy(bf16[64,3,128]{2,0,1:T(8,128)(2,1)} %bitcast.4) | data formatting | bytes 98304
